TPU v7x, 128 devices: a whole 4x4x4 slice. The times are simulated.
128 devices in a mesh: fsdp: 4 (over y_lo, core), ctx: 8 (over y_hi, z), tp: 4 (over x).
Axes of the slice: x: 4, y: 4 (y_hi: 2, y_lo: 2; y = y_hi * 2 + y_lo), z: 4, core: 2. Of those that a mesh axis runs over, the one named last changes fastest.
Arguments:
- layer_input: bfloat16 [16, 2048, 768], P('fsdp', 'ctx'), may hold values from -6 to 6
- segment_ids: int32 [16, 2048], P('fsdp', 'ctx'), may hold values from 0 to 3, never falling along the last dimension, each value on 1 to 1280 neighbouring positions
- proj_weight: bfloat16 [3, 768, 768], P(None, 'fsdp', 'tp'), may hold values from -0.21875 to 0.21875
- proj_bias: bfloat16 [2, 768], P(None, 'tp'), may hold values from -3 to 3
- out_weight: bfloat16 [768, 768], P('tp', 'fsdp'), may hold values from -2.5 to 2.5
- out_bias: bfloat16 [768], P('fsdp'), may hold values from -3 to 3
- first_gain: bfloat16 [768], P('fsdp'), may hold values from 0.099609375 to 1.8984375
- first_shift: bfloat16 [768], P('fsdp'), may hold values from -2 to 2
- up_weight: bfloat16 [768, 3072], P('fsdp', 'tp'), may hold values from -0.21875 to 0.21875
- up_bias: bfloat16 [3072], P('tp'), may hold values from -3 to 3
- down_weight: bfloat16 [3072, 768], P('tp', 'fsdp'), may hold values from -0.15625 to 0.15625
- down_bias: bfloat16 [768], P('fsdp'), may hold values from -2 to 2
- second_gain: bfloat16 [768], P('fsdp'), may hold values from 0.099609375 to 1.8984375
- second_shift: bfloat16 [768], P('fsdp'), may hold values from -2 to 2
- cotangent: bfloat16 [16, 2048, 768], P('fsdp', 'ctx'), may hold values from -6 to 6
Outputs:
- layer_output: bfloat16 [16, 2048, 768], P('fsdp', 'ctx')
- input_grad: float32 [16, 2048, 768], P('fsdp', 'ctx')
- proj_grad: float32 [3, 768, 768], P(None, ('fsdp', 'ctx'), 'tp')
- proj_bias_grad: float32 [2, 768], P(None, 'tp')
- out_grad: float32 [768, 768], P('tp', ('fsdp', 'ctx'))
- out_bias_grad: float32 [768], P(('fsdp', 'ctx'))
- first_gain_grad: float32 [768], P(('fsdp', 'ctx'))
- first_shift_grad: float32 [768], P(('fsdp', 'ctx'))
- up_grad: float32 [768, 3072], P(('fsdp', 'ctx'), 'tp')
- up_bias_grad: float32 [3072], P('tp')
- down_grad: float32 [3072, 768], P('tp', ('fsdp', 'ctx'))
- down_bias_grad: float32 [768], P(('fsdp', 'ctx'))
- second_gain_grad: float32 [768], P(('fsdp', 'ctx'))
- second_shift_grad: float32 [768], P(('fsdp', 'ctx'))
Inputs may be any that keep to these rules, and one draw needn't show every extreme that they name: `segment_ids`: ids never fall along a sequence; every document spans 1 to 1280 positions, and one in each sequence spans exactly 1280.
All inputs are finite; a program needn't handle non-finite values.
Results may differ from a plain program's by a relative error of at most 0.039.
Values may be sent and summed in bfloat16 or wider, within the bound.
A program may use at most 192 MiB of HBM per device.

v0:
```python
import jax
import jax.numpy as jnp
from jax import lax
from jax.sharding import PartitionSpec as P

HEAD_DIM = 64
norm_eps = 1e-12
masked_score = -1e30


def turned_gather(arrays, axis, dims):
    turned = [jnp.moveaxis(a, dim, 0) for a, dim in zip(arrays, dims)]
    widths = [t[0].size for t in turned]
    both = jnp.concatenate([t.reshape(-1, w) for t, w in zip(turned, widths)], axis=1)
    out = lax.all_gather(both, axis, axis=0, tiled=True)
    pieces = jnp.split(out, [sum(widths[:k]) for k in range(1, len(widths))], axis=1)
    return tuple(
        (
            jnp.moveaxis(b.reshape(-1, *t.shape[1:]), 0, dim)
            for b, t, dim in zip(pieces, turned, dims)
        )
    )


def sent_together(arrays, axis, dim, along):
    ends, at = ([], 0)
    for a in arrays[:-1]:
        at += a.shape[along]
        ends.append(at)
    both = jnp.concatenate(arrays, axis=along)
    return tuple(jnp.split(lax.all_gather(both, axis, axis=dim, tiled=True), ends, axis=along))


def rows_for(lines, count):
    spare = -len(lines) % count
    return jnp.pad(lines, [(0, spare)] + [(0, 0)] * (lines.ndim - 1))


def sum_by_parts(x, axis):
    lines = x.reshape(-1, *x.shape[1:][-1:])
    padded = rows_for(lines, lax.axis_size(axis))
    own = lax.psum_scatter(padded, axis, scatter_dimension=0, tiled=True)
    whole = lax.all_gather(own, axis, axis=0, tiled=True)
    return whole[: len(lines)].reshape(x.shape)


def cut_along(x, dim, count):
    shape = x.shape
    pieces = x.reshape(*shape[:dim], count, shape[dim] // count, *shape[dim + 1 :])
    return jnp.moveaxis(pieces, dim, 0)


def sum_together(arrays, axis, dims):
    count = lax.axis_size(axis)
    pieces = [cut_along(a, dim, count) for a, dim in zip(arrays, dims)]
    lines = jnp.concatenate([b.reshape(count, -1) for b in pieces], axis=1)
    width = max(16, -(-lines.shape[1] // 1024) * 8)
    lines = jnp.pad(lines, ((0, 0), (0, width * 128 - lines.shape[1]))).reshape(-1, 128)
    flat, at, outs = (lax.psum_scatter(lines, axis, tiled=True).reshape(-1), 0, [])
    for b in pieces:
        part = b[0]
        outs.append(flat[at : at + part.size].reshape(part.shape))
        at += part.size
    return tuple(outs)


def sent_to_all(x, axis):
    count = lax.axis_size(axis)
    return lax.all_to_all(jnp.broadcast_to(x[None], (count, *x.shape)), axis, 0, 0, tiled=True)


def of_everyone(x, axis):
    return sent_to_all(x, axis).sum(axis=0)


def packed_total(arrays, axis):
    ends = [0]
    for a in arrays:
        ends.append(ends[-1] + a.size)
    subtotal = of_everyone(jnp.concatenate([a.ravel() for a in arrays]), axis)
    return tuple((subtotal[b:e].reshape(a.shape) for a, b, e in zip(arrays, ends, ends[1:])))


def layer_norm(values_in, gain, shift):
    centre = jnp.mean(values_in, axis=-1, keepdims=True)
    centred = values_in - centre
    spread = jnp.mean(centred * centred, axis=-1, keepdims=True)
    return centred * lax.rsqrt(spread + norm_eps) * gain + shift


def gelu_exact(values_in):
    return jax.nn.gelu(values_in, approximate=False)


def doc_scores(queries, key_rows, query_docs, key_docs):
    raw_scores = jnp.einsum(
        "sqhd,skhd->shqk", queries, key_rows, preferred_element_type=jnp.float32
    ) * HEAD_DIM ** (-0.5)
    same_doc = query_docs[:, None, :, None] == key_docs[:, None, None, :]
    return (raw_scores, same_doc)


def whole_attention(queries, key_rows, value_rows, query_docs, key_docs):
    raw_scores, same_doc = doc_scores(queries, key_rows, query_docs, key_docs)
    row_high = jnp.max(jnp.where(same_doc, raw_scores, masked_score), axis=-1, keepdims=True)
    exp_terms = jnp.where(same_doc, jnp.exp(raw_scores - row_high), 0.0)
    row_total = jnp.sum(exp_terms, axis=-1, keepdims=True)
    attn_probs = (exp_terms / row_total).astype(jnp.bfloat16)
    attended = jnp.einsum(
        "shqk,skhd->sqhd", attn_probs, value_rows, preferred_element_type=jnp.float32
    )
    return (attended, row_high + jnp.log(row_total))


def queries_back(queries, key_rows, value_rows, query_docs, key_docs, log_total, grad_context):
    raw_scores, same_doc = doc_scores(queries, key_rows, query_docs, key_docs)
    attn_probs = jnp.where(same_doc, jnp.exp(raw_scores - log_total), 0.0)
    grad_probs = jnp.einsum(
        "sqhd,skhd->shqk", grad_context, value_rows, preferred_element_type=jnp.float32
    )
    row_delta = jnp.sum(attn_probs * grad_probs, axis=-1, keepdims=True)
    grad_scores = (attn_probs * (grad_probs - row_delta)).astype(jnp.bfloat16)
    grad_queries = jnp.einsum(
        "shqk,skhd->sqhd", grad_scores, key_rows, preferred_element_type=jnp.float32
    ) * HEAD_DIM ** (-0.5)
    return (grad_queries, row_delta)


def keys_back(
    all_queries,
    own_keys,
    own_values,
    all_query_docs,
    own_docs,
    all_log_total,
    all_delta,
    all_grad_context,
):
    raw_scores, same_doc = doc_scores(all_queries, own_keys, all_query_docs, own_docs)
    attn_probs = jnp.where(same_doc, jnp.exp(raw_scores - all_log_total), 0.0)
    probs_low = attn_probs.astype(jnp.bfloat16)
    grad_probs = jnp.einsum(
        "sqhd,skhd->shqk", all_grad_context, own_values, preferred_element_type=jnp.float32
    )
    grad_scores = (attn_probs * (grad_probs - all_delta)).astype(jnp.bfloat16)
    grad_keys = jnp.einsum(
        "shqk,sqhd->skhd", grad_scores, all_queries, preferred_element_type=jnp.float32
    ) * HEAD_DIM ** (-0.5)
    grad_values = jnp.einsum(
        "shqk,sqhd->skhd", probs_low, all_grad_context, preferred_element_type=jnp.float32
    )
    return (grad_keys, grad_values)


def shards(
    layer_input,
    segment_ids,
    proj_weight,
    proj_bias,
    out_weight,
    out_bias,
    first_gain,
    first_shift,
    up_weight,
    up_bias,
    down_weight,
    down_bias,
    second_gain,
    second_shift,
    cotangent,
):
    seq_count, group_len, model_width = layer_input.shape
    local_cols = proj_weight.shape[2]
    head_count = local_cols // HEAD_DIM
    row_count = seq_count * group_len
    (
        proj_full,
        out_full,
        up_full,
        down_full,
        out_shift,
        down_shift,
        gain_one,
        shift_one,
        gain_two,
        shift_two,
    ) = turned_gather(
        (
            proj_weight,
            out_weight,
            up_weight,
            down_weight,
            out_bias,
            down_bias,
            first_gain,
            first_shift,
            second_gain,
            second_shift,
        ),
        "fsdp",
        (1, 1, 0, 1, 0, 0, 0, 0, 0, 0),
    )
    gain_one = gain_one.astype(jnp.float32)
    shift_one = shift_one.astype(jnp.float32)
    gain_two = gain_two.astype(jnp.float32)
    shift_two = shift_two.astype(jnp.float32)
    flat_rows = layer_input.reshape(row_count, model_width)
    bias_pair = proj_bias.astype(jnp.float32)
    proj_pre = jnp.einsum("rd,tdc->trc", flat_rows, proj_full, preferred_element_type=jnp.float32)
    head_shape = (seq_count, group_len, head_count, HEAD_DIM)
    queries = (proj_pre[0] + bias_pair[0]).astype(jnp.bfloat16).reshape(head_shape)
    key_rows = proj_pre[1].astype(jnp.bfloat16).reshape(head_shape)
    value_rows = (proj_pre[2] + bias_pair[1]).astype(jnp.bfloat16).reshape(head_shape)
    all_keys, all_values, all_docs = (
        *sent_together((key_rows, value_rows), "ctx", 1, 0),
        lax.all_gather(segment_ids, "ctx", axis=1, tiled=True),
    )
    attended, log_total = whole_attention(queries, all_keys, all_values, segment_ids, all_docs)
    context = attended.reshape(row_count, local_cols).astype(jnp.bfloat16)
    attn_part = jnp.dot(context, out_full, preferred_element_type=jnp.float32)
    attn_full = lax.psum(attn_part.astype(jnp.bfloat16), "tp").astype(jnp.float32)
    first_sum = flat_rows.astype(jnp.float32) + attn_full + out_shift.astype(jnp.float32)
    first_norm = layer_norm(first_sum, gain_one, shift_one)
    norm_low = first_norm.astype(jnp.bfloat16)
    up_pre = jnp.dot(norm_low, up_full, preferred_element_type=jnp.float32) + up_bias.astype(
        jnp.float32
    )
    activated = gelu_exact(up_pre).astype(jnp.bfloat16)
    ffn_part = jnp.dot(activated, down_full, preferred_element_type=jnp.float32)
    ffn_full = lax.psum(ffn_part.astype(jnp.bfloat16), "tp").astype(jnp.float32)
    second_sum = first_norm + ffn_full + down_shift.astype(jnp.float32)
    second_norm, second_pull = jax.vjp(layer_norm, second_sum, gain_two, shift_two)
    layer_output = second_norm.astype(jnp.bfloat16).reshape(seq_count, group_len, model_width)
    grad_second, grad_gain_two, grad_shift_two = second_pull(
        cotangent.reshape(row_count, model_width).astype(jnp.float32)
    )
    grad_down_bias = jnp.sum(grad_second, axis=0)
    second_low = grad_second.astype(jnp.bfloat16)
    grad_down = jnp.einsum("rf,rd->fd", activated, second_low, preferred_element_type=jnp.float32)
    grad_active = jnp.einsum(
        "rd,fd->rf", second_low, down_full, preferred_element_type=jnp.float32
    ).astype(jnp.bfloat16)
    gelu_value, gelu_pull = jax.vjp(gelu_exact, up_pre)
    grad_up_pre = gelu_pull(grad_active.astype(jnp.float32))[0]
    grad_up_bias = jnp.sum(grad_up_pre, axis=0)
    up_low = grad_up_pre.astype(jnp.bfloat16)
    grad_up = jnp.einsum("rd,rf->df", norm_low, up_low, preferred_element_type=jnp.float32)
    norm_part = jnp.einsum("rf,df->rd", up_low, up_full, preferred_element_type=jnp.float32)
    grad_norm = grad_second + lax.psum(norm_part.astype(jnp.bfloat16), "tp").astype(jnp.float32)
    first_value, first_pull = jax.vjp(layer_norm, first_sum, gain_one, shift_one)
    grad_first, grad_gain_one, grad_shift_one = first_pull(grad_norm)
    grad_out_bias = jnp.sum(grad_first, axis=0)
    first_low = grad_first.astype(jnp.bfloat16)
    grad_out = jnp.einsum("rc,rd->cd", context, first_low, preferred_element_type=jnp.float32)
    grad_context = (
        jnp.einsum("rd,cd->rc", first_low, out_full, preferred_element_type=jnp.float32)
        .astype(jnp.bfloat16)
        .reshape(head_shape)
    )
    back_keys, back_values, back_docs = (all_keys, all_values, all_docs)
    grad_queries, row_delta = queries_back(
        queries, back_keys, back_values, segment_ids, back_docs, log_total, grad_context
    )
    all_queries, all_grad_context, all_query_docs = (
        *sent_together((queries, grad_context), "ctx", 1, 0),
        lax.all_gather(segment_ids, "ctx", axis=1, tiled=True),
    )
    all_log_total, all_delta = sent_together((log_total, row_delta), "ctx", 2, 0)
    grad_keys, grad_values = keys_back(
        all_queries,
        key_rows,
        value_rows,
        all_query_docs,
        segment_ids,
        all_log_total,
        all_delta,
        all_grad_context,
    )
    grad_query_flat = grad_queries.reshape(row_count, local_cols)
    grad_value_flat = grad_values.reshape(row_count, local_cols)
    grad_proj_bias = jnp.stack([jnp.sum(grad_query_flat, axis=0), jnp.sum(grad_value_flat, axis=0)])
    grad_stack = jnp.stack(
        [grad_query_flat, grad_keys.reshape(row_count, local_cols), grad_value_flat]
    ).astype(jnp.bfloat16)
    grad_proj = jnp.einsum("rd,trc->tdc", flat_rows, grad_stack, preferred_element_type=jnp.float32)
    input_part = jnp.einsum(
        "trc,tdc->rd", grad_stack, proj_full, preferred_element_type=jnp.float32
    )
    input_grad = (
        grad_first + sum_by_parts(input_part.astype(jnp.bfloat16), "tp").astype(jnp.float32)
    ).reshape(seq_count, group_len, model_width)
    (
        proj_grad,
        out_grad,
        up_grad,
        down_grad,
        out_bias_grad,
        down_bias_grad,
        first_gain_grad,
        first_shift_grad,
        second_gain_grad,
        second_shift_grad,
    ) = tuple(
        (
            part.astype(jnp.float32)
            for part in sum_together(
                (
                    grad_proj.astype(jnp.bfloat16),
                    grad_out.astype(jnp.bfloat16),
                    grad_up.astype(jnp.bfloat16),
                    grad_down.astype(jnp.bfloat16),
                    grad_out_bias.astype(jnp.bfloat16),
                    grad_down_bias.astype(jnp.bfloat16),
                    grad_gain_one.astype(jnp.bfloat16),
                    grad_shift_one.astype(jnp.bfloat16),
                    grad_gain_two.astype(jnp.bfloat16),
                    grad_shift_two.astype(jnp.bfloat16),
                ),
                ("fsdp", "ctx"),
                (1, 1, 0, 1, 0, 0, 0, 0, 0, 0),
            )
        )
    )
    proj_bias_grad, up_bias_grad = packed_total((grad_proj_bias, grad_up_bias), ("fsdp", "ctx"))
    return (
        layer_output,
        input_grad,
        proj_grad,
        proj_bias_grad,
        out_grad,
        out_bias_grad,
        first_gain_grad,
        first_shift_grad,
        up_grad,
        up_bias_grad,
        down_grad,
        down_bias_grad,
        second_gain_grad,
        second_shift_grad,
    )


def solution(mesh):
    placed = (
        P("fsdp", "ctx", None),
        P("fsdp", "ctx"),
        P(None, "fsdp", "tp"),
        P(None, "tp"),
        P("tp", "fsdp"),
        P("fsdp"),
        P("fsdp"),
        P("fsdp"),
        P("fsdp", "tp"),
        P("tp"),
        P("tp", "fsdp"),
        P("fsdp"),
        P("fsdp"),
        P("fsdp"),
        P("fsdp", "ctx", None),
    )
    return jax.shard_map(
        shards,
        mesh=mesh,
        in_specs=placed,
        out_specs=(
            P("fsdp", "ctx", None),
            P("fsdp", "ctx", None),
            P(None, ("fsdp", "ctx"), "tp"),
            P(None, "tp"),
            P("tp", ("fsdp", "ctx")),
            P(("fsdp", "ctx")),
            P(("fsdp", "ctx")),
            P(("fsdp", "ctx")),
            P(("fsdp", "ctx"), "tp"),
            P("tp"),
            P("tp", ("fsdp", "ctx")),
            P(("fsdp", "ctx")),
            P(("fsdp", "ctx")),
            P(("fsdp", "ctx")),
        ),
        check_vma=False,
    )
```

profile of v0, /device:TPU:1, one launch (start us, length us, event | category | flops | bytes accessed | tf_op | source)
XLA Modules:
  0.0 778.4 jit_solution(16677096041173922460)
XLA Ops:
  17.5 46.3 %all-gather.5.cloned.1.call-done = bf16[768,2310]{1,0:T(8,128)(2,1)} async-done(((bf16[192,2310]{1,0:T(8,128)(2,1)}), bf16[768,2310]{1,0:T(8,128)(2,1)}) %all-gather.5.cloned.1.call-update) | async-done | bytes 3548176 | tf_op jit(solution)/shard_map/all_gather | solution.py:15
  70.7 28.1 %all_gather.21 = s32[4,2048]{1,0:T(4,128)S(1)} all-gather(s32[4,256]{1,0:T(4,128)S(1)} %copy-done.34), channel_id=1, replica_groups=mesh['fsdp'=4,'ctx'=8,'tp'=4] {'ctx'}, dimensions={1}, use_global_device_ids=true | all-gather | bytes 36864 | tf_op jit(solution)/shard_map/all_gather | solution.py:216
  102.5 62.1 %all-gather.7.cloned.1.call-done = bf16[8,2048,3,64]{1,3,2,0:T(8,128)(2,1)} async-done(((bf16[8,256,3,64]{1,3,2,0:T(8,128)(2,1)}), bf16[8,2048,3,64]{1,3,2,0:T(8,128)(2,1)}) %all-gather.7.cloned.1.call-update) | async-done | bytes 6291472 | tf_op jit(solution)/shard_map/all_gather | solution.py:31
  164.5 12.8 %select_reduce_fusion = (f32[4,3,256]{2,1,0:T(4,128)S(1)}, f32[4,3,256,2048]{3,2,1,0:T(8,128)}) fusion(pred[4,256,2048]{2,1,0:T(8,128)(4,1)S(1)} %broadcast_compare_fusion.1, bf16[4,256,3,64]{1,3,2,0:T(8,128)(2,1)S(1)} %fusion.49, bf16[8,2048,3,64]{1,3,2,0:T(8,128)(2,1)} %all-gather.7.cloned.1.call-done), kind=kOutput, calls=%fused_computation.7 | convolution fusion | flops 824177664 | bytes 30814208 | tf_op jit(solution)/shard_map/sqhd,skhd->shqk/dot_general | solution.py:96
  177.3 12.0 %fusion = f32[4,3,256]{2,1,0:T(4,128)S(1)} fusion(f32[4,3,256,2048]{3,2,1,0:T(8,128)} %get-tuple-element.114, f32[4,3,256]{2,1,0:T(4,128)S(1)} %get-tuple-element.113, pred[4,256,2048]{2,1,0:T(8,128)(4,1)S(1)} %broadcast_compare_fusion.1), kind=kLoop, calls=%fused_computation.8 | loop fusion | flops 25162752 | bytes 27287552 | tf_op jit(solution)/shard_map/reduce_sum | solution.py:107
  189.3 13.3 %fusion.42 = bf16[4,256,3,64]{1,3,2,0:T(8,128)(2,1)S(1)} fusion(bf16[8,2048,3,64]{1,3,2,0:T(8,128)(2,1)} %all-gather.7.cloned.1.call-done, f32[4,3,256,2048]{3,2,1,0:T(8,128)} %get-tuple-element.114, f32[4,3,256]{2,1,0:T(4,128)S(1)} %fusion, f32[4,3,256]{2,1,0:T(4,128)S(1)} %get-tuple-element.113, pred[4,256,2048]{2,1,0:T(8,128)(4,1)S(1)} %broadcast_compare_fusion.1), kind=kOutput, calls=%fused_computation.90 | convolution fusion | flops 836960256 | bytes 33972224 | tf_op jit(solution)/shard_map/shqk,skhd->sqhd/dot_general | solution.py:109
  209.6 45.9 %all-reduce.7.cloned.1.call-done = bf16[1024,768]{1,0:T(8,128)(2,1)} async-done(((bf16[1024,768]{1,0:T(8,128)(2,1)}), bf16[1024,768]{1,0:T(8,128)(2,1)}) %all-reduce.7.cloned.1.call-update) | async-done | bytes 1572880 | tf_op jit(solution)/shard_map/psum | solution.py:221
  260.1 9.6 %multiply_convert_fusion.4 = (bf16[1024,768]{1,0:T(8,128)(2,1)S(1)}, f32[1024,768]{1,0:T(8,128)}, f32[1024,768]{1,0:T(8,128)}) fusion(f32[768]{0:T(1024)S(1)} %convert_element_type.279, bf16[768,2310]{1,0:T(8,128)(2,1)S(1)} %copy-done.21, f32[1024,768]{1,0:T(8,128)S(1)} %get-tuple-element.93, f32[768]{0:T(1024)S(1)} %get-tuple-element.78, ...), kind=kOutput, calls=%fused_computation.49 | convolution fusion | flops 1263009792 | bytes 12206080 | tf_op jit(solution)/shard_map/dot_general | solution.py:225
  273.8 50.4 %all-reduce.9.cloned.1.call-done = bf16[1024,768]{1,0:T(8,128)(2,1)} async-done(((bf16[1024,768]{1,0:T(8,128)(2,1)}), bf16[1024,768]{1,0:T(8,128)(2,1)}) %all-reduce.9.cloned.1.call-update) | async-done | bytes 1572880 | tf_op jit(solution)/shard_map/psum | solution.py:230
  340.3 50.6 %all-reduce.11.cloned.1.call-done = bf16[1024,768]{1,0:T(8,128)(2,1)} async-done(((bf16[1024,768]{1,0:T(8,128)(2,1)}), bf16[1024,768]{1,0:T(8,128)(2,1)}) %all-reduce.11.cloned.1.call-update) | async-done | bytes 1572880 | tf_op jit(solution)/shard_map/psum | solution.py:249
  390.9 4.4 multiply_reduce_fusion.1
  407.6 4.9 broadcast_compare_fusion
  413.2 4.2 convolution_convert_fusion.5
  420.0 21.4 %multiply_reduce_fusion = (f32[4,3,256]{2,1,0:T(4,128)S(1)}, f32[4,3,256,2048]{3,2,1,0:T(8,128)}) fusion(f32[4,3,256,2048]{3,2,1,0:T(8,128)} %get-tuple-element.114, f32[4,3,256]{2,1,0:T(4,128)S(1)} %log_add_fusion, pred[4,256,2048]{2,1,0:T(8,128)(4,1)} %copy-done.1, bf16[8,2048,3,64]{1,3,2,0:T(8,128)(2,1)} %all-gather.7.cloned.1.call-done, ...), kind=kOutput, calls=%fused_computation.3 | convolution fusion | flops 836760576 | bytes 55992320 | tf_op jit(solution)/shard_map/sqhd,skhd->shqk/dot_general | solution.py:118
  441.5 19.5 %fusion.77 = (f32[3,64]{1,0:T(4,128)}, bf16[4,256,3,64]{1,3,2,0:T(8,128)(2,1)S(1)}) fusion(bf16[8,2048,3,64]{1,3,2,0:T(8,128)(2,1)S(1)} %bitcast.94, f32[4,3,256,2048]{3,2,1,0:T(8,128)} %get-tuple-element.117, f32[4,3,256,2048]{3,2,1,0:T(8,128)} %get-tuple-element.114, f32[4,3,256]{2,1,0:T(4,128)S(1)} %get-tuple-element.116, ...), kind=kOutput, calls=%fused_computation.166 | convolution fusion | flops 843644736 | bytes 59138816 | tf_op jit(solution)/shard_map/shqk,skhd->sqhd/dot_general | solution.py:123
  461.6 30.1 %all_gather.23 = f32[8,3,2048,1]{2,1,0,3:T(4,128)S(1)} all-gather(f32[8,3,256,1]{2,1,0,3:T(4,128)S(1)} %pad_maximum_fusion.2), channel_id=1, replica_groups=mesh['fsdp'=4,'ctx'=8,'tp'=4] {'ctx'}, dimensions={2}, use_global_device_ids=true | all-gather | bytes 221184 | tf_op jit(solution)/shard_map/all_gather | solution.py:31
  492.5 8.1 %all-gather.9.cloned.1.call-done = bf16[8,2048,3,64]{1,3,2,0:T(8,128)(2,1)} async-done(((bf16[8,256,3,64]{1,3,2,0:T(8,128)(2,1)}), bf16[8,2048,3,64]{1,3,2,0:T(8,128)(2,1)}) %all-gather.9.cloned.1.call-update) | async-done | bytes 6291472 | tf_op jit(solution)/shard_map/all_gather | solution.py:31
  500.6 12.3 %fusion.80 = f32[4,3,2048,256]{3,2,1,0:T(8,128)} fusion(bf16[8,2048,3,64]{1,3,2,0:T(8,128)(2,1)} %all-gather.9.cloned.1.call-done, bf16[4,256,3,64]{1,3,2,0:T(8,128)(2,1)S(1)} %copy-done.18), kind=kOutput, calls=%fused_computation.169 | convolution fusion | flops 805306368 | bytes 31850496 | tf_op jit(solution)/shard_map/sqhd,skhd->shqk/dot_general | solution.py:142
  512.9 10.1 %fusion.66 = f32[4,3,2048,256]{3,2,1,0:T(8,128)} fusion(bf16[8,2048,3,64]{1,3,2,0:T(8,128)(2,1)S(1)} %copy-done, bf16[4,256,3,64]{1,0,3,2:T(4,128)(2,1)S(1)} %copy-done.16), kind=kOutput, calls=%fused_computation.159 | convolution fusion | flops 805306368 | bytes 31850496 | tf_op jit(solution)/shard_map/sqhd,skhd->shqk/dot_general | solution.py:96
  523.0 16.5 %fusion.43 = bf16[4,256,3,64]{1,3,2,0:T(8,128)(2,1)S(1)} fusion(bf16[8,2048,3,64]{1,3,2,0:T(8,128)(2,1)S(1)} %copy-done, f32[4,3,2048,256]{3,2,1,0:T(8,128)} %fusion.80, f32[4,3,2048,256]{3,2,1,0:T(8,128)} %fusion.66, f32[4,3,2048]{2,1,0:T(4,128)S(1)} %get-tuple-element.106, f32[4,3,2048]{2,1,0:T(4,128)S(1)} %get-tuple-element.105, ...), kind=kOutput, calls=%fused_computation.91 | convolution fusion | flops 843448320 | bytes 59310080 | tf_op jit(solution)/shard_map/shqk,sqhd->skhd/dot_general | solution.py:146
  540.1 12.0 %fusion.78 = (f32[3,64]{1,0:T(4,128)}, bf16[4,256,3,64]{1,3,2,0:T(8,128)(2,1)S(1)}) fusion(bf16[8,2048,3,64]{1,3,2,0:T(8,128)(2,1)} %all-gather.9.cloned.1.call-done, f32[4,3,2048,256]{3,2,1,0:T(8,128)} %fusion.66, f32[4,3,2048]{2,1,0:T(4,128)S(1)} %get-tuple-element.105, pred[4,2048,256]{2,1,0:T(8,128)(4,1)S(1)} %copy-done.3), kind=kOutput, calls=%fused_computation.167 | convolution fusion | flops 830865216 | bytes 34046720 | tf_op jit(solution)/shard_map/shqk,sqhd->skhd/dot_general | solution.py:149
  554.3 4.3 bitcast_convert_fusion
  558.9 4.0 convolution_convert_fusion.4
  562.9 6.3 copy.144
  569.1 13.0 %reshape.337 = bf16[32,18432]{1,0:T(8,128)(2,1)} reshape(bf16[32,768,24]{2,1,0:T(8,128)(2,1)} %bitcast.95) | data formatting | bytes 2359296 | tf_op jit(solution)/shard_map/reshape | solution.py:56
  591.3 3.8 fusion.33
  609.5 21.0 %all-gather.11.cloned.1.call-done = bf16[1024,768]{1,0:T(8,128)(2,1)} async-done(((bf16[256,768]{1,0:T(8,128)(2,1)}), bf16[1024,768]{1,0:T(8,128)(2,1)}) %all-gather.11.cloned.1.call-update) | async-done | bytes 1572880 | tf_op jit(solution)/shard_map/all_gather | solution.py:43
  643.0 4.1 pad.4
  647.1 5.2 reshape.338
  654.0 7.7 all-to-all-start
  662.9 6.3 all-to-all-done
  670.6 93.9 %all-reduce.13.cloned.1.call-done = bf16[14080,128]{1,0:T(8,128)(2,1)} async-done(((bf16[14080,128]{1,0:T(8,128)(2,1)}), bf16[14080,128]{1,0:T(8,128)(2,1)}) %all-reduce.13.cloned.1.call-update) | async-done | bytes 3604496
  (236 shorter events, 118.8 us)
Async XLA Ops:
  7.2 10.2 %copy-start.43 = (bf16[2,192]{1,0:T(2,128)(2,1)S(1)}, bf16[2,192]{1,0:T(2,128)(2,1)}, u32[]{:S(2)}) copy-start(bf16[2,192]{1,0:T(2,128)(2,1)} %param.18) | copy-start | bytes 2308
  7.2 56.6 %all-gather.5.cloned.1.call-start = ((), (), s32[]{:S(2)}) async-start(), calls=%async_computation.2 | async-start | bytes 4669440 | tf_op jit(solution)/shard_map/all_gather | solution.py:15
  14.1 51.7 %copy-start.10 = (bf16[4,256,768]{2,1,0:T(8,128)(2,1)S(1)}, bf16[4,256,768]{2,1,0:T(8,128)(2,1)}, u32[]{:S(2)}) copy-start(bf16[4,256,768]{2,1,0:T(8,128)(2,1)} %param.15) | copy-start | bytes 4718596
  17.3 147.2 %all-gather.7.cloned.1.call-start = ((), (), s32[]{:S(2)}) async-start(), calls=%async_computation.3 | async-start | bytes 7077888 | tf_op jit(solution)/shard_map/all_gather | solution.py:31
  70.6 184.9 %all-reduce.7.cloned.1.call-start = ((), (), s32[]{:S(2)}) async-start(), calls=%async_computation.4 | async-start | bytes 3145728 | tf_op jit(solution)/shard_map/psum | solution.py:221
  100.2 89.1 %copy-start.1 = (pred[4,256,2048]{2,1,0:T(8,128)(4,1)}, pred[4,256,2048]{2,1,0:T(8,128)(4,1)S(1)}, u32[]{:S(2)}) copy-start(pred[4,256,2048]{2,1,0:T(8,128)(4,1)S(1)} %broadcast_compare_fusion.1) | copy-start | bytes 6291460
  102.4 74.9 %copy-start.23 = (bf16[4,256,3,64]{1,3,2,0:T(8,128)(2,1)}, bf16[4,256,3,64]{1,3,2,0:T(8,128)(2,1)S(1)}, u32[]{:S(2)}) copy-start(bf16[4,256,3,64]{1,3,2,0:T(8,128)(2,1)S(1)} %fusion.49) | copy-start | bytes 1179652
  177.3 12.0 %copy-start.30 = (f32[4,3,256]{2,1,0:T(4,128)}, f32[4,3,256]{2,1,0:T(4,128)S(1)}, u32[]{:S(2)}) copy-start(f32[4,3,256]{2,1,0:T(4,128)S(1)} %get-tuple-element.113) | copy-start | bytes 36868
  189.3 13.4 %copy-start.31 = (f32[4,3,256]{2,1,0:T(4,128)}, f32[4,3,256]{2,1,0:T(4,128)S(1)}, u32[]{:S(2)}) copy-start(f32[4,3,256]{2,1,0:T(4,128)S(1)} %fusion) | copy-start | bytes 36868
  203.0 52.5 %copy-start.11 = (bf16[4,256,768]{2,1,0:T(8,128)(2,1)S(1)}, bf16[4,256,768]{2,1,0:T(8,128)(2,1)}, u32[]{:S(2)}) copy-start(bf16[4,256,768]{2,1,0:T(8,128)(2,1)} %param.15) | copy-start | bytes 4718596
  206.9 117.3 %all-reduce.9.cloned.1.call-start = ((), (), s32[]{:S(2)}) async-start(), calls=%async_computation.5 | async-start | bytes 3145728 | tf_op jit(solution)/shard_map/psum | solution.py:230
  209.6 114.6 %copy-start.36 = (f32[768]{0:T(1024)}, f32[768]{0:T(1024)S(1)}, u32[]{:S(2)}) copy-start(f32[768]{0:T(1024)S(1)} %get-tuple-element.78) | copy-start | bytes 9220
  209.6 185.7 %copy-start.26 = (f32[768]{0:T(1024)}, f32[768]{0:T(1024)S(1)}, u32[]{:S(2)}) copy-start(f32[768]{0:T(1024)S(1)} %get-tuple-element.79) | copy-start | bytes 9220
  260.1 135.2 %copy-start.27 = (f32[1024]{0:T(1024)}, f32[1024]{0:T(1024)S(1)}, u32[]{:S(2)}) copy-start(f32[1024]{0:T(1024)S(1)} %fusion.55) | copy-start | bytes 12292
  273.5 117.4 %all-reduce.11.cloned.1.call-start = ((), (), s32[]{:S(2)}) async-start(), calls=%async_computation.6 | async-start | bytes 3145728 | tf_op jit(solution)/shard_map/psum | solution.py:249
  332.4 62.9 %copy-start.32 = (f32[1024]{0:T(1024)}, f32[1024]{0:T(1024)S(1)}, u32[]{:S(2)}) copy-start(f32[1024]{0:T(1024)S(1)} %negate_multiply_fusion.2) | copy-start | bytes 12292
  340.2 160.3 %all-gather.9.cloned.1.call-start = ((), (), s32[]{:S(2)}) async-start(), calls=%async_computation.7 | async-start | bytes 7077888 | tf_op jit(solution)/shard_map/all_gather | solution.py:31
  404.7 200.9 %reduce-scatter.2.cloned.1.call-start = ((), (), s32[]{:S(2)}) async-start(), calls=%async_computation.8 | async-start | bytes 1966080 | tf_op jit(solution)/shard_map/reduce_scatter | solution.py:42
  417.4 24.1 %slice-start = ((s8[6291456]{0:T(1024)(128)(4,1)}), s8[2097152]{0:T(1024)(128)(4,1)S(1)}, s32[]{:S(2)}) async-start(s8[6291456]{0:T(1024)(128)(4,1)} %bitcast.93), calls=%async_computation.11 | async-start | bytes 4194304
  420.0 21.5 %slice-start.1 = ((s8[6291456]{0:T(1024)(128)(4,1)}), s8[4194304]{0:T(1024)(128)(4,1)S(1)}, s32[]{:S(2)}) async-start(s8[6291456]{0:T(1024)(128)(4,1)} %bitcast.93), calls=%async_computation.12 | async-start | bytes 8388608
  420.0 21.5 %copy-start.2 = (pred[4,256,2048]{2,1,0:T(8,128)(4,1)S(1)}, pred[4,256,2048]{2,1,0:T(8,128)(4,1)}, u32[]{:S(2)}) copy-start(pred[4,256,2048]{2,1,0:T(8,128)(4,1)} %copy-done.1) | copy-start | bytes 6291460
  461.0 39.6 %copy-start.18 = (bf16[4,256,3,64]{1,3,2,0:T(8,128)(2,1)S(1)}, bf16[4,256,3,64]{1,3,2,0:T(8,128)(2,1)}, u32[]{:S(2)}) copy-start(bf16[4,256,3,64]{1,3,2,0:T(8,128)(2,1)} %copy-done.17) | copy-start | bytes 1179652
  492.5 20.4 %copy-start.16 = (bf16[4,256,3,64]{1,0,3,2:T(4,128)(2,1)S(1)}, bf16[4,256,3,64]{1,0,3,2:T(4,128)(2,1)}, u32[]{:S(2)}) copy-start(bf16[4,256,3,64]{1,0,3,2:T(4,128)(2,1)} %copy-done.15) | copy-start | bytes 1179652
  500.6 12.3 %copy-start = (bf16[8,2048,3,64]{1,3,2,0:T(8,128)(2,1)S(1)}, bf16[8,2048,3,64]{1,3,2,0:T(8,128)(2,1)}, u32[]{:S(2)}) copy-start(bf16[8,2048,3,64]{1,3,2,0:T(8,128)(2,1)} %all-gather.9.cloned.1.call-done) | copy-start | bytes 18874372
  558.6 71.9 %all-gather.11.cloned.1.call-start = ((), (), s32[]{:S(2)}) async-start(), calls=%async_computation.9 | async-start | bytes 1966080 | tf_op jit(solution)/shard_map/all_gather | solution.py:43
  569.1 13.0 %copy-start.37 = (bf16[768]{0:T(1024)(128)(2,1)S(1)}, bf16[768]{0:T(1024)(128)(2,1)}, u32[]{:S(2)}) copy-start(bf16[768]{0:T(1024)(128)(2,1)} %get-tuple-element.72) | copy-start | bytes 4612
  569.1 13.1 %copy-start.5 = (f32[1024,768]{1,0:T(8,128)S(1)}, f32[1024,768]{1,0:T(8,128)}, u32[]{:S(2)}) copy-start(f32[1024,768]{1,0:T(8,128)} %copy-done.4) | copy-start | bytes 9437188
  569.1 13.1 %copy-start.20 = (bf16[24,8,4,256]{3,1,2,0:T(8,128)(2,1)S(1)}, bf16[24,8,4,256]{3,1,2,0:T(8,128)(2,1)}, u32[]{:S(2)}) copy-start(bf16[24,8,4,256]{3,1,2,0:T(8,128)(2,1)} %copy-done.19) | copy-start | bytes 1179652
  569.1 13.2 %copy-start.29 = (f32[1024]{0:T(1024)S(1)}, f32[1024]{0:T(1024)}, u32[]{:S(2)}) copy-start(f32[1024]{0:T(1024)} %copy-done.28) | copy-start | bytes 12292
  605.7 158.9 %all-reduce.13.cloned.1.call-start = ((), (), s32[]{:S(2)}) async-start(), calls=%async_computation.10 | async-start | bytes 7208960
  609.5 32.0 %copy-start.35 = (bf16[32,24]{1,0:T(8,128)(2,1)S(1)}, bf16[32,24]{1,0:T(8,128)(2,1)}, u32[]{:S(2)}) copy-start(bf16[32,24]{1,0:T(8,128)(2,1)} %convert_element_type.320) | copy-start | bytes 4612
  654.0 15.3 %all-to-all-start = ((f32[32,1,1152]{2,1,0:T(1,128)}), f32[32,1,1152]{2,1,0:T(1,128)S(1)}, u32[]{:S(2)}, u32[]{:S(2)}) async-start(f32[32,1,1152]{2,1,0:T(1,128)} %broadcast_in_dim.87), calls=%async_computation.1 | async-start | bytes 294912 | tf_op jit(solution)/shard_map/all_to_all | solution.py:69
  (29 other events, 90.8 us)
Sparse Core Ops, SparseCore 0:
  17.4 46.3 all-gather.4
  70.7 93.7 all-gather.6
  207.0 48.4 all-reduce.6
  273.6 50.4 all-reduce.8
  340.3 50.4 all-reduce.10
  404.8 95.7 all-gather.8
  558.7 22.8 reduce-scatter.1
  605.8 24.6 all-gather.10
  652.4 112.0 all-reduce.12
where the time goes:
time: 784 us; the launch traced here: 778 us
  waiting for transfers between devices  385 us (49%)
  matrix products  160 us (20%)
  local copies, waits for them, and re-layouts  99.4 us (13%)
  blocking collectives  58.2 us (7%)
  other arithmetic  50.8 us (6%)
  between operations  15.6 us (2%)
  starting transfers between devices  9.47 us (1%)
    unnamed x10, waiting for transfers between devices  94.1 us
    all_gather x2, waiting for transfers between devices, sent_together(): lax.all_gather(both, axis, axis=dim, tiled=True)  70.2 us
    psum x1, waiting for transfers between devices, shards(): lax.psum(norm_part.astype(jnp.bfloat16), 'tp').astype(jnp.float32)  50.6 us
    psum x1, waiting for transfers between devices, shards(): ffn_full = lax.psum(ffn_part.astype(jnp.bfloat16), 'tp').astype(jnp.float32)  50.4 us
    all_gather x1, waiting for transfers between devices, turned_gather(): out = lax.all_gather(both, axis, axis=0, tiled=True)  46.3 us
    psum x1, waiting for transfers between devices, shards(): lax.psum(attn_part.astype(jnp.bfloat16), 'tp').astype(jnp.float32)  45.9 us
    all_gather x1, blocking collectives, sent_together(): lax.all_gather(both, axis, axis=dim, tiled=True)  30.1 us
    all_gather x1, blocking collectives, shards(): lax.all_gather(segment_ids, 'ctx', axis=1, tiled=True)  28.1 us
  transfers between devices with their start and end apart: 10, of which 9 were waited for; matrix products, arithmetic and copies ran while one was open for 15% of the time, Pallas kernels for 0%

commit v1 on v0

--- a/solution.py
+++ b/solution.py
@@ -213,7 +213,9 @@
     value_rows = (proj_pre[2] + bias_pair[1]).astype(jnp.bfloat16).reshape(head_shape)
     all_keys, all_values, all_docs = (
         *sent_together((key_rows, value_rows), "ctx", 1, 0),
-        lax.all_gather(segment_ids, "ctx", axis=1, tiled=True),
+        jnp.concatenate(
+            lax.all_to_all(jnp.stack([segment_ids] * lax.axis_size("ctx")), "ctx", 0, 0), axis=1
+        ),
     )
     attended, log_total = whole_attention(queries, all_keys, all_values, segment_ids, all_docs)
     context = attended.reshape(row_count, local_cols).astype(jnp.bfloat16)

time: 784 us -> 815 us (1.040)
  waiting for transfers between devices: 385 us -> 411 us
    all_gather x1, waiting for transfers between devices: 21 us -> 34.6 us  [sum_by_parts(): whole = lax.all_gather(own, axis, axis=0, tiled=True)]
    unnamed x118 -> x116, local copies, waits for them, and re-layouts: 26.6 us -> 26.6 us
  transfers between devices with their start and end apart: 10 -> 11, of which waited for: 9 -> 9; matrix products, arithmetic and copies ran while one was open for 15% -> 14% of each run, Pallas kernels for 0% -> 0%
where the time goes in v1:
time: 815 us; the launch traced here: 810 us
  waiting for transfers between devices  411 us (50%)
  matrix products  160 us (20%)
  local copies, waits for them, and re-layouts  100 us (12%)
  blocking collectives  57.3 us (7%)
  other arithmetic  50 us (6%)
  between operations  15.6 us (2%)
  starting transfers between devices  15.5 us (2%)
    unnamed x10, waiting for transfers between devices  94.1 us
    all_gather x2, waiting for transfers between devices, sent_together(): lax.all_gather(both, axis, axis=dim, tiled=True)  76.7 us
    psum x1, waiting for transfers between devices, shards(): lax.psum(norm_part.astype(jnp.bfloat16), 'tp').astype(jnp.float32)  50.6 us
    psum x1, waiting for transfers between devices, shards(): ffn_full = lax.psum(ffn_part.astype(jnp.bfloat16), 'tp').astype(jnp.float32)  50.3 us
    all_gather x1, waiting for transfers between devices, turned_gather(): out = lax.all_gather(both, axis, axis=0, tiled=True)  46.3 us
    psum x1, waiting for transfers between devices, shards(): lax.psum(attn_part.astype(jnp.bfloat16), 'tp').astype(jnp.float32)  45.8 us
    all_gather x1, waiting for transfers between devices, sum_by_parts(): whole = lax.all_gather(own, axis, axis=0, tiled=True)  34.6 us
    all_gather x1, blocking collectives, shards(): lax.all_gather(segment_ids, 'ctx', axis=1, tiled=True)  28.7 us
  transfers between devices with their start and end apart: 11, of which 9 were waited for; matrix products, arithmetic and copies ran while one was open for 14% of the time, Pallas kernels for 0%

profile of v1, /device:TPU:1, one launch (start us, length us, event | category | flops | bytes accessed | tf_op | source)
XLA Modules:
  0.0 809.6 jit_solution(3039817415467251341)
XLA Ops:
  17.5 46.3 %all-gather.5.cloned.1.call-done = bf16[768,2310]{1,0:T(8,128)(2,1)} async-done(((bf16[192,2310]{1,0:T(8,128)(2,1)}), bf16[768,2310]{1,0:T(8,128)(2,1)}) %all-gather.5.cloned.1.call-update) | async-done | bytes 3548176 | tf_op jit(solution)/shard_map/all_gather | solution.py:15
  71.2 6.3 all-to-all-start
  77.8 6.3 all-to-all-done
  87.8 76.7 %all-gather.7.cloned.1.call-done = bf16[8,2048,3,64]{1,3,2,0:T(8,128)(2,1)} async-done(((bf16[8,256,3,64]{1,3,2,0:T(8,128)(2,1)}), bf16[8,2048,3,64]{1,3,2,0:T(8,128)(2,1)}) %all-gather.7.cloned.1.call-update) | async-done | bytes 6291472 | tf_op jit(solution)/shard_map/all_gather | solution.py:31
  164.4 12.8 %select_reduce_fusion = (f32[4,3,256]{2,1,0:T(4,128)S(1)}, f32[4,3,256,2048]{3,2,1,0:T(8,128)}) fusion(pred[4,256,2048]{2,1,0:T(8,128)(4,1)S(1)} %broadcast_compare_fusion.1, bf16[4,256,3,64]{1,3,2,0:T(8,128)(2,1)S(1)} %fusion.49, bf16[8,2048,3,64]{1,3,2,0:T(8,128)(2,1)} %all-gather.7.cloned.1.call-done), kind=kOutput, calls=%fused_computation.7 | convolution fusion | flops 824177664 | bytes 30814208 | tf_op jit(solution)/shard_map/sqhd,skhd->shqk/dot_general | solution.py:96
  177.2 12.0 %fusion = f32[4,3,256]{2,1,0:T(4,128)S(1)} fusion(f32[4,3,256,2048]{3,2,1,0:T(8,128)} %get-tuple-element.114, f32[4,3,256]{2,1,0:T(4,128)S(1)} %get-tuple-element.113, pred[4,256,2048]{2,1,0:T(8,128)(4,1)S(1)} %broadcast_compare_fusion.1), kind=kLoop, calls=%fused_computation.8 | loop fusion | flops 25162752 | bytes 27287552 | tf_op jit(solution)/shard_map/reduce_sum | solution.py:107
  189.2 13.3 %fusion.42 = bf16[4,256,3,64]{1,3,2,0:T(8,128)(2,1)S(1)} fusion(bf16[8,2048,3,64]{1,3,2,0:T(8,128)(2,1)} %all-gather.7.cloned.1.call-done, f32[4,3,256,2048]{3,2,1,0:T(8,128)} %get-tuple-element.114, f32[4,3,256]{2,1,0:T(4,128)S(1)} %fusion, f32[4,3,256]{2,1,0:T(4,128)S(1)} %get-tuple-element.113, pred[4,256,2048]{2,1,0:T(8,128)(4,1)S(1)} %broadcast_compare_fusion.1), kind=kOutput, calls=%fused_computation.90 | convolution fusion | flops 836960256 | bytes 33972224 | tf_op jit(solution)/shard_map/shqk,skhd->sqhd/dot_general | solution.py:109
  209.6 45.8 %all-reduce.7.cloned.1.call-done = bf16[1024,768]{1,0:T(8,128)(2,1)} async-done(((bf16[1024,768]{1,0:T(8,128)(2,1)}), bf16[1024,768]{1,0:T(8,128)(2,1)}) %all-reduce.7.cloned.1.call-update) | async-done | bytes 1572880 | tf_op jit(solution)/shard_map/psum | solution.py:223
  260.0 9.6 %multiply_convert_fusion.4 = (bf16[1024,768]{1,0:T(8,128)(2,1)S(1)}, f32[1024,768]{1,0:T(8,128)}, f32[1024,768]{1,0:T(8,128)}) fusion(f32[768]{0:T(1024)S(1)} %convert_element_type.279, bf16[768,2310]{1,0:T(8,128)(2,1)S(1)} %copy-done.21, f32[1024,768]{1,0:T(8,128)S(1)} %get-tuple-element.93, f32[768]{0:T(1024)S(1)} %get-tuple-element.78, ...), kind=kOutput, calls=%fused_computation.49 | convolution fusion | flops 1263009792 | bytes 12206080 | tf_op jit(solution)/shard_map/dot_general | solution.py:227
  273.7 50.3 %all-reduce.9.cloned.1.call-done = bf16[1024,768]{1,0:T(8,128)(2,1)} async-done(((bf16[1024,768]{1,0:T(8,128)(2,1)}), bf16[1024,768]{1,0:T(8,128)(2,1)}) %all-reduce.9.cloned.1.call-update) | async-done | bytes 1572880 | tf_op jit(solution)/shard_map/psum | solution.py:232
  340.2 50.6 %all-reduce.11.cloned.1.call-done = bf16[1024,768]{1,0:T(8,128)(2,1)} async-done(((bf16[1024,768]{1,0:T(8,128)(2,1)}), bf16[1024,768]{1,0:T(8,128)(2,1)}) %all-reduce.11.cloned.1.call-update) | async-done | bytes 1572880 | tf_op jit(solution)/shard_map/psum | solution.py:251
  390.8 4.4 multiply_reduce_fusion.1
  407.0 28.7 %all_gather.21 = s32[4,2048]{1,0:T(4,128)S(1)} all-gather(s32[4,256]{1,0:T(4,128)S(1)} %copy-done.29), channel_id=1, replica_groups=mesh['fsdp'=4,'ctx'=8,'tp'=4] {'ctx'}, dimensions={1}, use_global_device_ids=true | all-gather | bytes 36864 | tf_op jit(solution)/shard_map/all_gather | solution.py:268
  435.7 4.0 broadcast_compare_fusion
  440.5 4.1 convolution_convert_fusion.5
  447.2 22.1 %multiply_reduce_fusion = (f32[4,3,256]{2,1,0:T(4,128)S(1)}, f32[4,3,256,2048]{3,2,1,0:T(8,128)}) fusion(f32[4,3,256,2048]{3,2,1,0:T(8,128)} %get-tuple-element.114, f32[4,3,256]{2,1,0:T(4,128)S(1)} %log_add_fusion, pred[4,256,2048]{2,1,0:T(8,128)(4,1)} %copy-done.1, bf16[8,2048,3,64]{1,3,2,0:T(8,128)(2,1)} %all-gather.7.cloned.1.call-done, ...), kind=kOutput, calls=%fused_computation.3 | convolution fusion | flops 836760576 | bytes 55992320 | tf_op jit(solution)/shard_map/sqhd,skhd->shqk/dot_general | solution.py:118
  469.3 18.7 %fusion.77 = (f32[3,64]{1,0:T(4,128)}, bf16[4,256,3,64]{1,3,2,0:T(8,128)(2,1)S(1)}) fusion(bf16[8,2048,3,64]{1,3,2,0:T(8,128)(2,1)S(1)} %bitcast.97, f32[4,3,256,2048]{3,2,1,0:T(8,128)} %get-tuple-element.117, f32[4,3,256,2048]{3,2,1,0:T(8,128)} %get-tuple-element.114, f32[4,3,256]{2,1,0:T(4,128)S(1)} %get-tuple-element.116, ...), kind=kOutput, calls=%fused_computation.166 | convolution fusion | flops 843644736 | bytes 59138816 | tf_op jit(solution)/shard_map/shqk,skhd->sqhd/dot_general | solution.py:123
  488.6 28.6 %all_gather.22 = f32[8,3,2048,1]{2,1,0,3:T(4,128)S(1)} all-gather(f32[8,3,256,1]{2,1,0,3:T(4,128)S(1)} %pad_maximum_fusion.2), channel_id=1, replica_groups=mesh['fsdp'=4,'ctx'=8,'tp'=4] {'ctx'}, dimensions={2}, use_global_device_ids=true | all-gather | bytes 221184 | tf_op jit(solution)/shard_map/all_gather | solution.py:31
  518.1 12.3 %fusion.80 = f32[4,3,2048,256]{3,2,1,0:T(8,128)} fusion(bf16[8,2048,3,64]{1,3,2,0:T(8,128)(2,1)} %all-gather.9.cloned.1.call-done, bf16[4,256,3,64]{1,3,2,0:T(8,128)(2,1)S(1)} %copy-done.18), kind=kOutput, calls=%fused_computation.169 | convolution fusion | flops 805306368 | bytes 31850496 | tf_op jit(solution)/shard_map/sqhd,skhd->shqk/dot_general | solution.py:142
  530.4 10.1 %fusion.66 = f32[4,3,2048,256]{3,2,1,0:T(8,128)} fusion(bf16[8,2048,3,64]{1,3,2,0:T(8,128)(2,1)S(1)} %copy-done, bf16[4,256,3,64]{1,0,3,2:T(4,128)(2,1)S(1)} %copy-done.16), kind=kOutput, calls=%fused_computation.159 | convolution fusion | flops 805306368 | bytes 31850496 | tf_op jit(solution)/shard_map/sqhd,skhd->shqk/dot_general | solution.py:96
  540.5 16.5 %fusion.43 = bf16[4,256,3,64]{1,3,2,0:T(8,128)(2,1)S(1)} fusion(bf16[8,2048,3,64]{1,3,2,0:T(8,128)(2,1)S(1)} %copy-done, f32[4,3,2048,256]{3,2,1,0:T(8,128)} %fusion.80, f32[4,3,2048,256]{3,2,1,0:T(8,128)} %fusion.66, f32[4,3,2048]{2,1,0:T(4,128)S(1)} %get-tuple-element.106, f32[4,3,2048]{2,1,0:T(4,128)S(1)} %get-tuple-element.105, ...), kind=kOutput, calls=%fused_computation.91 | convolution fusion | flops 843448320 | bytes 59310080 | tf_op jit(solution)/shard_map/shqk,sqhd->skhd/dot_general | solution.py:146
  557.6 12.0 %fusion.78 = (f32[3,64]{1,0:T(4,128)}, bf16[4,256,3,64]{1,3,2,0:T(8,128)(2,1)S(1)}) fusion(bf16[8,2048,3,64]{1,3,2,0:T(8,128)(2,1)} %all-gather.9.cloned.1.call-done, f32[4,3,2048,256]{3,2,1,0:T(8,128)} %fusion.66, f32[4,3,2048]{2,1,0:T(4,128)S(1)} %get-tuple-element.105, pred[4,2048,256]{2,1,0:T(8,128)(4,1)S(1)} %copy-done.3), kind=kOutput, calls=%fused_computation.167 | convolution fusion | flops 830865216 | bytes 34046720 | tf_op jit(solution)/shard_map/shqk,sqhd->skhd/dot_general | solution.py:149
  571.8 4.3 bitcast_convert_fusion
  576.4 4.0 convolution_convert_fusion.4
  580.4 6.3 copy.144
  586.7 13.0 %reshape.343 = bf16[32,18432]{1,0:T(8,128)(2,1)} reshape(bf16[32,768,24]{2,1,0:T(8,128)(2,1)} %bitcast.98) | data formatting | bytes 2359296 | tf_op jit(solution)/shard_map/reshape | solution.py:56
  627.2 34.6 %all-gather.11.cloned.1.call-done = bf16[1024,768]{1,0:T(8,128)(2,1)} async-done(((bf16[256,768]{1,0:T(8,128)(2,1)}), bf16[1024,768]{1,0:T(8,128)(2,1)}) %all-gather.11.cloned.1.call-update) | async-done | bytes 1572880 | tf_op jit(solution)/shard_map/all_gather | solution.py:43
  674.2 4.1 pad.4
  678.3 5.2 reshape.344
  685.2 7.7 all-to-all-start.1
  694.1 6.3 all-to-all-done.1
  701.8 94.0 %all-reduce.13.cloned.1.call-done = bf16[14080,128]{1,0:T(8,128)(2,1)} async-done(((bf16[14080,128]{1,0:T(8,128)(2,1)}), bf16[14080,128]{1,0:T(8,128)(2,1)}) %all-reduce.13.cloned.1.call-update) | async-done | bytes 3604496
  (237 shorter events, 123.0 us)
Async XLA Ops:
  7.2 56.6 %all-gather.5.cloned.1.call-start = ((), (), s32[]{:S(2)}) async-start(), calls=%async_computation.3 | async-start | bytes 4669440 | tf_op jit(solution)/shard_map/all_gather | solution.py:15
  14.1 51.7 %copy-start.10 = (bf16[4,256,768]{2,1,0:T(8,128)(2,1)S(1)}, bf16[4,256,768]{2,1,0:T(8,128)(2,1)}, u32[]{:S(2)}) copy-start(bf16[4,256,768]{2,1,0:T(8,128)(2,1)} %param.15) | copy-start | bytes 4718596
  17.3 147.1 %all-gather.7.cloned.1.call-start = ((), (), s32[]{:S(2)}) async-start(), calls=%async_computation.4 | async-start | bytes 7077888 | tf_op jit(solution)/shard_map/all_gather | solution.py:31
  68.6 15.6 %copy-start.15 = (bf16[4,256,3,64]{1,0,3,2:T(4,128)(2,1)}, bf16[4,256,3,64]{1,0,3,2:T(4,128)(2,1)S(1)}, u32[]{:S(2)}) copy-start(bf16[4,256,3,64]{1,0,3,2:T(4,128)(2,1)S(1)} %convert_element_type.262) | copy-start | bytes 1179652
  71.2 12.9 %all-to-all-start = ((s32[8,4,256]{2,1,0:T(4,128)}), s32[8,4,256]{2,1,0:T(4,128)S(1)}, u32[]{:S(2)}, u32[]{:S(2)}) async-start(s32[8,4,256]{2,1,0:T(4,128)} %stack.11), calls=%async_computation | async-start | bytes 65536 | tf_op jit(solution)/shard_map/all_to_all | solution.py:217
  77.5 177.8 %all-reduce.7.cloned.1.call-start = ((), (), s32[]{:S(2)}) async-start(), calls=%async_computation.5 | async-start | bytes 3145728 | tf_op jit(solution)/shard_map/psum | solution.py:223
  85.5 103.7 %copy-start.1 = (pred[4,256,2048]{2,1,0:T(8,128)(4,1)}, pred[4,256,2048]{2,1,0:T(8,128)(4,1)S(1)}, u32[]{:S(2)}) copy-start(pred[4,256,2048]{2,1,0:T(8,128)(4,1)S(1)} %broadcast_compare_fusion.1) | copy-start | bytes 6291460
  87.8 89.5 %copy-start.23 = (bf16[4,256,3,64]{1,3,2,0:T(8,128)(2,1)}, bf16[4,256,3,64]{1,3,2,0:T(8,128)(2,1)S(1)}, u32[]{:S(2)}) copy-start(bf16[4,256,3,64]{1,3,2,0:T(8,128)(2,1)S(1)} %fusion.49) | copy-start | bytes 1179652
  189.2 13.4 %copy-start.31 = (f32[4,3,256]{2,1,0:T(4,128)}, f32[4,3,256]{2,1,0:T(4,128)S(1)}, u32[]{:S(2)}) copy-start(f32[4,3,256]{2,1,0:T(4,128)S(1)} %fusion) | copy-start | bytes 36868
  202.9 52.5 %copy-start.11 = (bf16[4,256,768]{2,1,0:T(8,128)(2,1)S(1)}, bf16[4,256,768]{2,1,0:T(8,128)(2,1)}, u32[]{:S(2)}) copy-start(bf16[4,256,768]{2,1,0:T(8,128)(2,1)} %param.15) | copy-start | bytes 4718596
  206.8 117.3 %all-reduce.9.cloned.1.call-start = ((), (), s32[]{:S(2)}) async-start(), calls=%async_computation.6 | async-start | bytes 3145728 | tf_op jit(solution)/shard_map/psum | solution.py:232
  209.6 114.5 %copy-start.35 = (f32[768]{0:T(1024)}, f32[768]{0:T(1024)S(1)}, u32[]{:S(2)}) copy-start(f32[768]{0:T(1024)S(1)} %get-tuple-element.78) | copy-start | bytes 9220
  209.6 185.6 %copy-start.25 = (f32[768]{0:T(1024)}, f32[768]{0:T(1024)S(1)}, u32[]{:S(2)}) copy-start(f32[768]{0:T(1024)S(1)} %get-tuple-element.79) | copy-start | bytes 9220
  260.0 135.2 %copy-start.26 = (f32[1024]{0:T(1024)}, f32[1024]{0:T(1024)S(1)}, u32[]{:S(2)}) copy-start(f32[1024]{0:T(1024)S(1)} %fusion.55) | copy-start | bytes 12292
  273.4 117.3 %all-reduce.11.cloned.1.call-start = ((), (), s32[]{:S(2)}) async-start(), calls=%async_computation.7 | async-start | bytes 3145728 | tf_op jit(solution)/shard_map/psum | solution.py:251
  332.3 62.9 %copy-start.32 = (f32[1024]{0:T(1024)}, f32[1024]{0:T(1024)S(1)}, u32[]{:S(2)}) copy-start(f32[1024]{0:T(1024)S(1)} %negate_multiply_fusion.2) | copy-start | bytes 12292
  340.1 177.9 %all-gather.9.cloned.1.call-start = ((), (), s32[]{:S(2)}) async-start(), calls=%async_computation.8 | async-start | bytes 7077888 | tf_op jit(solution)/shard_map/all_gather | solution.py:31
  404.6 218.7 %reduce-scatter.2.cloned.1.call-start = ((), (), s32[]{:S(2)}) async-start(), calls=%async_computation.9 | async-start | bytes 1966080 | tf_op jit(solution)/shard_map/reduce_scatter | solution.py:42
  444.6 24.7 %slice-start = ((s8[6291456]{0:T(1024)(128)(4,1)}), s8[2097152]{0:T(1024)(128)(4,1)S(1)}, s32[]{:S(2)}) async-start(s8[6291456]{0:T(1024)(128)(4,1)} %bitcast.96), calls=%async_computation.12 | async-start | bytes 4194304
  447.2 22.1 %slice-start.1 = ((s8[6291456]{0:T(1024)(128)(4,1)}), s8[4194304]{0:T(1024)(128)(4,1)S(1)}, s32[]{:S(2)}) async-start(s8[6291456]{0:T(1024)(128)(4,1)} %bitcast.96), calls=%async_computation.13 | async-start | bytes 8388608
  447.2 22.1 %copy-start.2 = (pred[4,256,2048]{2,1,0:T(8,128)(4,1)S(1)}, pred[4,256,2048]{2,1,0:T(8,128)(4,1)}, u32[]{:S(2)}) copy-start(pred[4,256,2048]{2,1,0:T(8,128)(4,1)} %copy-done.1) | copy-start | bytes 6291460
  488.0 30.0 %copy-start.18 = (bf16[4,256,3,64]{1,3,2,0:T(8,128)(2,1)S(1)}, bf16[4,256,3,64]{1,3,2,0:T(8,128)(2,1)}, u32[]{:S(2)}) copy-start(bf16[4,256,3,64]{1,3,2,0:T(8,128)(2,1)} %copy-done.17) | copy-start | bytes 1179652
  518.0 12.4 %copy-start.16 = (bf16[4,256,3,64]{1,0,3,2:T(4,128)(2,1)S(1)}, bf16[4,256,3,64]{1,0,3,2:T(4,128)(2,1)}, u32[]{:S(2)}) copy-start(bf16[4,256,3,64]{1,0,3,2:T(4,128)(2,1)} %copy-done.15) | copy-start | bytes 1179652
  518.1 12.3 %copy-start = (bf16[8,2048,3,64]{1,3,2,0:T(8,128)(2,1)S(1)}, bf16[8,2048,3,64]{1,3,2,0:T(8,128)(2,1)}, u32[]{:S(2)}) copy-start(bf16[8,2048,3,64]{1,3,2,0:T(8,128)(2,1)} %all-gather.9.cloned.1.call-done) | copy-start | bytes 18874372
  576.1 85.7 %all-gather.11.cloned.1.call-start = ((), (), s32[]{:S(2)}) async-start(), calls=%async_computation.10 | async-start | bytes 1966080 | tf_op jit(solution)/shard_map/all_gather | solution.py:43
  586.7 13.1 %copy-start.36 = (bf16[768]{0:T(1024)(128)(2,1)S(1)}, bf16[768]{0:T(1024)(128)(2,1)}, u32[]{:S(2)}) copy-start(bf16[768]{0:T(1024)(128)(2,1)} %get-tuple-element.72) | copy-start | bytes 4612
  586.7 13.1 %copy-start.5 = (f32[1024,768]{1,0:T(8,128)S(1)}, f32[1024,768]{1,0:T(8,128)}, u32[]{:S(2)}) copy-start(f32[1024,768]{1,0:T(8,128)} %copy-done.4) | copy-start | bytes 9437188
  586.7 13.2 %copy-start.20 = (bf16[24,8,4,256]{3,1,2,0:T(8,128)(2,1)S(1)}, bf16[24,8,4,256]{3,1,2,0:T(8,128)(2,1)}, u32[]{:S(2)}) copy-start(bf16[24,8,4,256]{3,1,2,0:T(8,128)(2,1)} %copy-done.19) | copy-start | bytes 1179652
  586.7 13.2 %copy-start.28 = (f32[1024]{0:T(1024)S(1)}, f32[1024]{0:T(1024)}, u32[]{:S(2)}) copy-start(f32[1024]{0:T(1024)} %copy-done.27) | copy-start | bytes 12292
  623.3 172.5 %all-reduce.13.cloned.1.call-start = ((), (), s32[]{:S(2)}) async-start(), calls=%async_computation.11 | async-start | bytes 7208960
  627.2 45.5 %copy-start.34 = (bf16[32,24]{1,0:T(8,128)(2,1)S(1)}, bf16[32,24]{1,0:T(8,128)(2,1)}, u32[]{:S(2)}) copy-start(bf16[32,24]{1,0:T(8,128)(2,1)} %convert_element_type.320) | copy-start | bytes 4612
  685.2 15.3 %all-to-all-start.1 = ((f32[32,1,1152]{2,1,0:T(1,128)}), f32[32,1,1152]{2,1,0:T(1,128)S(1)}, u32[]{:S(2)}, u32[]{:S(2)}) async-start(f32[32,1,1152]{2,1,0:T(1,128)} %broadcast_in_dim.85), calls=%async_computation.2 | async-start | bytes 294912 | tf_op jit(solution)/shard_map/all_to_all | solution.py:69
  (29 other events, 109.4 us)
Sparse Core Ops, SparseCore 0:
  17.4 46.3 all-gather.4
  70.7 93.6 all-gather.6
  206.9 48.4 all-reduce.6
  273.5 50.4 all-reduce.8
  340.2 50.4 all-reduce.10
  404.7 93.7 all-gather.8
  576.2 36.5 reduce-scatter.1
  623.4 38.3 all-gather.10
  683.6 112.1 all-reduce.12
